TPU v7x, 512 devices: a whole 4x8x8 slice. The times are simulated.
512 devices in a mesh: pb: 32 (over x, z), ao: 16 (over y, core).
Axes of the slice: x: 4, y: 8, z: 8, core: 2. Of those that a mesh axis runs over, the one named last changes fastest.
Arguments:
- queries: bfloat16 [32768, 128], P('pb'), may hold values from -4 to 4
- centres: bfloat16 [32768, 128], P(('pb', 'ao')), may hold values from -4 to 4
- coefs: bfloat16 [32768, 4096], P('pb', 'ao'), may hold values from -3 to 3
- pattern: int32 [32, 5], replicated, may hold values from 0 to 1, as said below
Outputs:
- scores: bfloat16 [32768, 4096], P('pb', 'ao')
Inputs may be any that keep to these rules, and one draw needn't show every extreme that they name: pattern[i, j] tells whether query block i lists centre block i + j - 2; it is 0 where that block lies outside 0 to 31, and 1 for j = 2.
All inputs are finite; a program needn't handle non-finite values.
Results may differ from a plain program's by a relative error of at most 0.0049.
Values may be sent and summed in bfloat16 or wider, within the bound.
A program may use at most 64 MiB of HBM per device.

v0:
```python
import math
import jax
import jax.numpy as jnp
from jax import lax
from jax.sharding import PartitionSpec as P

RADIUS_FACTOR = 1.3


def shifted(block, axis, distance):
    devices = range(lax.axis_size(axis))
    route = [(i - distance, i) for i in devices if i - distance in devices]
    return lax.ppermute(block, axis, route)


def query_norms(query_rows):
    query_wide = query_rows.astype(jnp.float32)
    return jnp.sum(query_wide * query_wide, axis=1)[:, None]


def wendland_block(query_rows, query_norm, centre_rows):
    centre_wide = centre_rows.astype(jnp.float32)
    centre_norm = jnp.sum(centre_wide * centre_wide, axis=1)[None, :]
    cross = jnp.dot(query_rows, centre_rows.T, preferred_element_type=jnp.float32)
    dist = jnp.sqrt(query_norm + centre_norm - 2.0 * cross)
    scaled = dist / (RADIUS_FACTOR * math.sqrt(query_rows.shape[1]))
    inner = jnp.maximum(1.0 - scaled, 0.0)
    return inner * inner * inner * inner * (4.0 * scaled + 1.0)


def contribute(query_rows, query_norm, centre_rows, coef_rows, weight):
    kern = (
        wendland_block(query_rows, query_norm, centre_rows) * weight.astype(jnp.float32)
    ).astype(jnp.bfloat16)
    return jnp.dot(kern, coef_rows, preferred_element_type=jnp.float32)


def per_device(queries, centres, coefs, pattern):
    band_width = pattern.shape[1]
    half_band = band_width // 2
    my_block = lax.axis_index("pb")
    my_pattern = lax.dynamic_index_in_dim(pattern, my_block, 0, keepdims=False)
    panel_coords = lax.all_gather(centres, "ao", axis=0, tiled=True)
    my_norm = query_norms(queries)
    offsets = [shift_by for shift_by in range(-half_band, half_band + 1) if shift_by != 0]
    accumulated = contribute(queries, my_norm, panel_coords, coefs, my_pattern[half_band])
    for shift_by in offsets:
        far_coords, far_coefs = shifted((panel_coords, coefs), "pb", -shift_by)
        accumulated = accumulated + contribute(
            queries, my_norm, far_coords, far_coefs, my_pattern[half_band + shift_by]
        )
    return accumulated.astype(jnp.bfloat16)


def solution(mesh):
    in_specs = (P("pb", None), P(("pb", "ao"), None), P("pb", "ao"), P())
    out_specs = P("pb", "ao")
    return jax.shard_map(
        per_device, mesh=mesh, in_specs=in_specs, out_specs=out_specs, check_vma=False
    )
```

profile of v0, /device:TPU:2, one launch (start us, length us, event | category | flops | bytes accessed | tf_op | source)
XLA Modules:
  0.0 104.8 jit_solution(7479997999850689913)
XLA Ops:
  0.0 0.0 copy-start
  0.0 18.7 %all_gather.3 = bf16[1024,128]{1,0:T(8,128)(2,1)S(1)} all-gather(bf16[64,128]{1,0:T(8,128)(2,1)} %param.5), channel_id=1, replica_groups=mesh['pb'=32,'ao'=16] {'ao'}, dimensions={0}, use_global_device_ids=true | all-gather | bytes 278528 | tf_op jit(solution)/shard_map/all_gather | solution.py:43
  18.7 10.9 %collective-permute-start.6 = (bf16[1024,128]{1,0:T(8,128)(2,1)S(1)}, bf16[1024,128]{1,0:T(8,128)(2,1)S(1)}, u32[]{:S(2)}, u32[]{:S(2)}) collective-permute-start(bf16[1024,128]{1,0:T(8,128)(2,1)S(1)} %all_gather.3), channel_id=1, source_target_pairs={{32,0},{48,16},{64,32},{80,48},{96,64},{112,80},{128,96},{144,112}... | collective-permute-start | bytes 786440 | tf_op jit(solution)/shard_map/ppermute | solution.py:13
  29.6 2.5 %collective-permute-start.4 = (bf16[1024,128]{1,0:T(8,128)(2,1)S(1)}, bf16[1024,128]{1,0:T(8,128)(2,1)S(1)}, u32[]{:S(2)}, u32[]{:S(2)}) collective-permute-start(bf16[1024,128]{1,0:T(8,128)(2,1)S(1)} %all_gather.3), channel_id=1, source_target_pairs={{16,0},{32,16},{48,32},{64,48},{80,64},{96,80},{112,96},{128,112},... | collective-permute-start | bytes 786440 | tf_op jit(solution)/shard_map/ppermute | solution.py:13
  32.0 3.4 %collective-permute-start.2 = (bf16[1024,128]{1,0:T(8,128)(2,1)S(1)}, bf16[1024,128]{1,0:T(8,128)(2,1)S(1)}, u32[]{:S(2)}, u32[]{:S(2)}) collective-permute-start(bf16[1024,128]{1,0:T(8,128)(2,1)S(1)} %all_gather.3), channel_id=1, source_target_pairs={{0,16},{16,32},{32,48},{48,64},{64,80},{80,96},{96,112},{112,128},... | collective-permute-start | bytes 786440 | tf_op jit(solution)/shard_map/ppermute | solution.py:13
  35.4 2.8 %collective-permute-start = (bf16[1024,128]{1,0:T(8,128)(2,1)S(1)}, bf16[1024,128]{1,0:T(8,128)(2,1)S(1)}, u32[]{:S(2)}, u32[]{:S(2)}) collective-permute-start(bf16[1024,128]{1,0:T(8,128)(2,1)S(1)} %all_gather.3), channel_id=1, source_target_pairs={{0,32},{16,48},{32,64},{48,80},{64,96},{80,112},{96,128},{112,144}... | collective-permute-start | bytes 786440 | tf_op jit(solution)/shard_map/ppermute | solution.py:13
  38.3 2.5 %collective-permute-start.3 = (bf16[1024,256]{1,0:T(8,128)(2,1)}, bf16[1024,256]{1,0:T(8,128)(2,1)S(1)}, u32[]{:S(2)}, u32[]{:S(2)}) collective-permute-start(bf16[1024,256]{1,0:T(8,128)(2,1)} %param.6), channel_id=1, source_target_pairs={{0,16},{16,32},{32,48},{48,64},{64,80},{80,96},{96,112},{112,128},... | collective-permute-start | bytes 1572872 | tf_op jit(solution)/shard_map/ppermute | solution.py:13
  40.7 0.2 multiply_reduce_fusion.4
  41.0 0.0 copy-done
  41.0 0.1 constant_dynamic-slice_fusion
  41.0 0.6 fusion.50
  42.4 1.2 %multiply_reduce_fusion.5 = f32[1024]{0:T(1024)S(1)} fusion(bf16[1024,128]{1,0:T(8,128)(2,1)} %param.4), kind=kLoop, calls=%fused_computation.35 | loop fusion | flops 392192 | bytes 266240 | tf_op jit(solution)/shard_map/reduce_sum | solution.py:18
  43.5 0.0 copy-start.2
  43.5 5.2 %fusion.19 = f32[1024,256]{1,0:T(8,128)} fusion(bf16[1024,256]{1,0:T(8,128)(2,1)} %param.6, bf16[1024,128]{1,0:T(8,128)(2,1)} %param.4, bf16[1024,128]{1,0:T(8,128)(2,1)S(1)} %all_gather.3, f32[]{:T(128)} %bitcast, f32[1024]{0:T(1024)S(1)} %multiply_reduce_fusion.4, f32[1024]{0:T(1024)S(1)} %multiply_reduce_fusion.5), kind=kOutput, calls=%fused_computation.24 | convolution fusion | flops 819986432 | bytes 2105348 | tf_op jit(solution)/shard_map/dot_general | solution.py:35
  48.8 0.0 copy-start.1
  51.4 0.0 collective-permute-done.6
  51.4 0.0 copy-done.2
  51.4 2.5 %collective-permute-start.1 = (bf16[1024,256]{1,0:T(8,128)(2,1)S(1)}, bf16[1024,256]{1,0:T(8,128)(2,1)S(1)}, u32[]{:S(2)}, u32[]{:S(2)}) collective-permute-start(bf16[1024,256]{1,0:T(8,128)(2,1)S(1)} %copy-done.2), channel_id=1, source_target_pairs={{0,32},{16,48},{32,64},{48,80},{64,96},{80,112},{96,128},{112,144}... | collective-permute-start | bytes 1572872 | tf_op jit(solution)/shard_map/ppermute | solution.py:13
  53.9 0.2 multiply_reduce_fusion
  54.1 0.0 collective-permute-done.4
  54.1 6.4 %collective-permute-start.7 = (bf16[1024,256]{1,0:T(8,128)(2,1)S(1)}, bf16[1024,256]{1,0:T(8,128)(2,1)}, u32[]{:S(2)}, u32[]{:S(2)}) collective-permute-start(bf16[1024,256]{1,0:T(8,128)(2,1)S(1)} %copy-done.2), channel_id=1, source_target_pairs={{32,0},{48,16},{64,32},{80,48},{96,64},{112,80},{128,96},{144,112}... | collective-permute-start | bytes 1572872 | tf_op jit(solution)/shard_map/ppermute | solution.py:13
  60.5 0.2 multiply_reduce_fusion.1
  60.7 0.0 collective-permute-done.2
  60.7 3.6 %collective-permute-start.5 = (bf16[1024,256]{1,0:T(8,128)(2,1)S(1)}, bf16[1024,256]{1,0:T(8,128)(2,1)}, u32[]{:S(2)}, u32[]{:S(2)}) collective-permute-start(bf16[1024,256]{1,0:T(8,128)(2,1)S(1)} %copy-done.2), channel_id=1, source_target_pairs={{16,0},{32,16},{48,32},{64,48},{80,64},{96,80},{112,96},{128,112},... | collective-permute-start | bytes 1572872 | tf_op jit(solution)/shard_map/ppermute | solution.py:13
  64.3 0.2 multiply_reduce_fusion.2
  64.5 0.0 collective-permute-done
  64.5 0.2 multiply_reduce_fusion.3
  64.7 13.2 %collective-permute-done.3 = bf16[1024,256]{1,0:T(8,128)(2,1)S(1)} collective-permute-done((bf16[1024,256]{1,0:T(8,128)(2,1)}, bf16[1024,256]{1,0:T(8,128)(2,1)S(1)}, u32[]{:S(2)}, u32[]{:S(2)}) %collective-permute-start.3) | collective-permute-done | bytes 524320 | tf_op jit(solution)/shard_map/ppermute | solution.py:13
  77.9 0.0 copy-done.1
  77.9 4.1 %fusion.17 = f32[1024,256]{1,0:T(8,128)} fusion(bf16[1024,256]{1,0:T(8,128)(2,1)S(1)} %collective-permute-done.3, bf16[1024,128]{1,0:T(8,128)(2,1)S(1)} %copy-done.1, bf16[1024,128]{1,0:T(8,128)(2,1)S(1)} %collective-permute-done.2, f32[]{:T(128)} %bitcast.2, f32[1024]{0:T(1024)S(1)} %multiply_reduce_fusion.2, f32[1024]{0:T(1024)S(1)} %multiply_reduce_fusion.5), kind=kOutput, calls=%fused_computation.22 | convolution fusion | flops 819986432 | bytes 2105348 | tf_op jit(solution)/shard_map/dot_general | solution.py:35
  82.0 1.8 %collective-permute-done.7 = bf16[1024,256]{1,0:T(8,128)(2,1)} collective-permute-done((bf16[1024,256]{1,0:T(8,128)(2,1)S(1)}, bf16[1024,256]{1,0:T(8,128)(2,1)}, u32[]{:S(2)}, u32[]{:S(2)}) %collective-permute-start.7) | collective-permute-done | bytes 524320 | tf_op jit(solution)/shard_map/ppermute | solution.py:13
  83.8 5.1 %fusion.15 = f32[1024,256]{1,0:T(8,128)} fusion(bf16[1024,256]{1,0:T(8,128)(2,1)} %collective-permute-done.7, bf16[1024,128]{1,0:T(8,128)(2,1)S(1)} %copy-done.1, bf16[1024,128]{1,0:T(8,128)(2,1)S(1)} %collective-permute-done.6, f32[]{:T(128)} %bitcast.4, f32[1024]{0:T(1024)S(1)} %multiply_reduce_fusion, f32[1024]{0:T(1024)S(1)} %multiply_reduce_fusion.5), kind=kOutput, calls=%fused_computation.20 | convolution fusion | flops 819986432 | bytes 2105348 | tf_op jit(solution)/shard_map/dot_general | solution.py:35
  88.9 5.2 %collective-permute-done.5 = bf16[1024,256]{1,0:T(8,128)(2,1)} collective-permute-done((bf16[1024,256]{1,0:T(8,128)(2,1)S(1)}, bf16[1024,256]{1,0:T(8,128)(2,1)}, u32[]{:S(2)}, u32[]{:S(2)}) %collective-permute-start.5) | collective-permute-done | bytes 524320 | tf_op jit(solution)/shard_map/ppermute | solution.py:13
  94.1 5.1 %fusion.16 = f32[1024,256]{1,0:T(8,128)} fusion(bf16[1024,256]{1,0:T(8,128)(2,1)} %collective-permute-done.5, bf16[1024,128]{1,0:T(8,128)(2,1)S(1)} %copy-done.1, bf16[1024,128]{1,0:T(8,128)(2,1)S(1)} %collective-permute-done.4, f32[]{:T(128)} %bitcast.3, f32[1024]{0:T(1024)S(1)} %multiply_reduce_fusion.1, f32[1024]{0:T(1024)S(1)} %multiply_reduce_fusion.5), kind=kOutput, calls=%fused_computation.21 | convolution fusion | flops 819986432 | bytes 2105348 | tf_op jit(solution)/shard_map/dot_general | solution.py:35
  99.2 0.0 collective-permute-done.1
  99.2 5.6 %fusion.24 = bf16[1024,256]{1,0:T(8,128)(2,1)} fusion(f32[1024,256]{1,0:T(8,128)} %fusion.15, f32[1024,256]{1,0:T(8,128)} %fusion.16, f32[1024,256]{1,0:T(8,128)} %fusion.17, f32[1024,256]{1,0:T(8,128)} %fusion.19, bf16[1024,256]{1,0:T(8,128)(2,1)S(1)} %collective-permute-done.1, bf16[1024,128]{1,0:T(8,128)(2,1)S(1)} %copy-done.1, ...), kind=kOutput, calls=%fused_computation.29 | convolution fusion | flops 821297152 | bytes 5775364 | tf_op jit(solution)/shard_map/dot_general | solution.py:35
Async XLA Ops:
  0.0 41.0 %copy-start = (s32[32,5]{0,1:T(8,128)S(1)}, s32[32,5]{0,1:T(8,128)}, u32[]{:S(2)}) copy-start(s32[32,5]{0,1:T(8,128)} %param.7) | copy-start | bytes 1924
  18.7 32.7 %collective-permute-start.6 = (bf16[1024,128]{1,0:T(8,128)(2,1)S(1)}, bf16[1024,128]{1,0:T(8,128)(2,1)S(1)}, u32[]{:S(2)}, u32[]{:S(2)}) collective-permute-start(bf16[1024,128]{1,0:T(8,128)(2,1)S(1)} %all_gather.3), channel_id=1, source_target_pairs={{32,0},{48,16},{64,32},{80,48},{96,64},{112,80},{128,96},{144,112}... | collective-permute-start | bytes 786440 | tf_op jit(solution)/shard_map/ppermute | solution.py:13
  29.6 24.6 %collective-permute-start.4 = (bf16[1024,128]{1,0:T(8,128)(2,1)S(1)}, bf16[1024,128]{1,0:T(8,128)(2,1)S(1)}, u32[]{:S(2)}, u32[]{:S(2)}) collective-permute-start(bf16[1024,128]{1,0:T(8,128)(2,1)S(1)} %all_gather.3), channel_id=1, source_target_pairs={{16,0},{32,16},{48,32},{64,48},{80,64},{96,80},{112,96},{128,112},... | collective-permute-start | bytes 786440 | tf_op jit(solution)/shard_map/ppermute | solution.py:13
  32.0 28.7 %collective-permute-start.2 = (bf16[1024,128]{1,0:T(8,128)(2,1)S(1)}, bf16[1024,128]{1,0:T(8,128)(2,1)S(1)}, u32[]{:S(2)}, u32[]{:S(2)}) collective-permute-start(bf16[1024,128]{1,0:T(8,128)(2,1)S(1)} %all_gather.3), channel_id=1, source_target_pairs={{0,16},{16,32},{32,48},{48,64},{64,80},{80,96},{96,112},{112,128},... | collective-permute-start | bytes 786440 | tf_op jit(solution)/shard_map/ppermute | solution.py:13
  35.4 29.1 %collective-permute-start = (bf16[1024,128]{1,0:T(8,128)(2,1)S(1)}, bf16[1024,128]{1,0:T(8,128)(2,1)S(1)}, u32[]{:S(2)}, u32[]{:S(2)}) collective-permute-start(bf16[1024,128]{1,0:T(8,128)(2,1)S(1)} %all_gather.3), channel_id=1, source_target_pairs={{0,32},{16,48},{32,64},{48,80},{64,96},{80,112},{96,128},{112,144}... | collective-permute-start | bytes 786440 | tf_op jit(solution)/shard_map/ppermute | solution.py:13
  38.3 39.7 %collective-permute-start.3 = (bf16[1024,256]{1,0:T(8,128)(2,1)}, bf16[1024,256]{1,0:T(8,128)(2,1)S(1)}, u32[]{:S(2)}, u32[]{:S(2)}) collective-permute-start(bf16[1024,256]{1,0:T(8,128)(2,1)} %param.6), channel_id=1, source_target_pairs={{0,16},{16,32},{32,48},{48,64},{64,80},{80,96},{96,112},{112,128},... | collective-permute-start | bytes 1572872 | tf_op jit(solution)/shard_map/ppermute | solution.py:13
  43.5 7.9 %copy-start.2 = (bf16[1024,256]{1,0:T(8,128)(2,1)S(1)}, bf16[1024,256]{1,0:T(8,128)(2,1)}, u32[]{:S(2)}) copy-start(bf16[1024,256]{1,0:T(8,128)(2,1)} %param.6) | copy-start | bytes 1572868
  48.8 29.2 %copy-start.1 = (bf16[1024,128]{1,0:T(8,128)(2,1)S(1)}, bf16[1024,128]{1,0:T(8,128)(2,1)}, u32[]{:S(2)}) copy-start(bf16[1024,128]{1,0:T(8,128)(2,1)} %param.4) | copy-start | bytes 786436
  51.4 47.8 %collective-permute-start.1 = (bf16[1024,256]{1,0:T(8,128)(2,1)S(1)}, bf16[1024,256]{1,0:T(8,128)(2,1)S(1)}, u32[]{:S(2)}, u32[]{:S(2)}) collective-permute-start(bf16[1024,256]{1,0:T(8,128)(2,1)S(1)} %copy-done.2), channel_id=1, source_target_pairs={{0,32},{16,48},{32,64},{48,80},{64,96},{80,112},{96,128},{112,144}... | collective-permute-start | bytes 1572872 | tf_op jit(solution)/shard_map/ppermute | solution.py:13
  54.1 29.7 %collective-permute-start.7 = (bf16[1024,256]{1,0:T(8,128)(2,1)S(1)}, bf16[1024,256]{1,0:T(8,128)(2,1)}, u32[]{:S(2)}, u32[]{:S(2)}) collective-permute-start(bf16[1024,256]{1,0:T(8,128)(2,1)S(1)} %copy-done.2), channel_id=1, source_target_pairs={{32,0},{48,16},{64,32},{80,48},{96,64},{112,80},{128,96},{144,112}... | collective-permute-start | bytes 1572872 | tf_op jit(solution)/shard_map/ppermute | solution.py:13
  60.7 33.4 %collective-permute-start.5 = (bf16[1024,256]{1,0:T(8,128)(2,1)S(1)}, bf16[1024,256]{1,0:T(8,128)(2,1)}, u32[]{:S(2)}, u32[]{:S(2)}) collective-permute-start(bf16[1024,256]{1,0:T(8,128)(2,1)S(1)} %copy-done.2), channel_id=1, source_target_pairs={{16,0},{32,16},{48,32},{64,48},{80,64},{96,80},{112,96},{128,112},... | collective-permute-start | bytes 1572872 | tf_op jit(solution)/shard_map/ppermute | solution.py:13
where the time goes:
time: 105 us
  starting transfers between devices  34.4 us (33%)
  matrix products  25.1 us (24%)
  waiting for transfers between devices  20.2 us (19%)
  blocking collectives  18.7 us (18%)
  between operations  3.51 us (3%)
  other arithmetic  2.2 us (2%)
    ppermute x8, starting transfers between devices, shifted(): return lax.ppermute(block, axis, route)  34.4 us
    dot_general x5, matrix products, contribute(): return jnp.dot(kern, coef_rows, preferred_element_type=jnp.float32)  25.1 us
    ppermute x8, waiting for transfers between devices, shifted(): return lax.ppermute(block, axis, route)  20.2 us
    all_gather x1, blocking collectives, per_device(): panel_coords = lax.all_gather(centres, 'ao', axis=0, tiled=True)  18.7 us
  transfers between devices with their start and end apart: 8, of which 3 were waited for; matrix products, arithmetic and copies ran while one was open for 21% of the time, Pallas kernels for 0%

commit v1 on v0

--- a/solution.py
+++ b/solution.py
@@ -40,7 +40,9 @@
     half_band = band_width // 2
     my_block = lax.axis_index("pb")
     my_pattern = lax.dynamic_index_in_dim(pattern, my_block, 0, keepdims=False)
-    panel_coords = lax.all_gather(centres, "ao", axis=0, tiled=True)
+    panel_coords = jnp.concatenate(
+        lax.all_to_all(jnp.stack([centres] * lax.axis_size("ao")), "ao", 0, 0), axis=0
+    )
     my_norm = query_norms(queries)
     offsets = [shift_by for shift_by in range(-half_band, half_band + 1) if shift_by != 0]
     accumulated = contribute(queries, my_norm, panel_coords, coefs, my_pattern[half_band])

time: 105 us -> 101 us (0.962)
  blocking collectives: 18.7 us -> 0 us
  starting transfers between devices: 34.4 us -> 43.3 us
  waiting for transfers between devices: 20.2 us -> 25.3 us
  local copies, waits for them, and re-layouts: 0.7 us -> 2.31 us
  matrix products: 25.1 us -> 24 us
    all_gather x1 -> x0, blocking collectives: 18.7 us -> none  [per_device(): panel_coords = lax.all_gather(centres, 'ao', axis=0, tiled=True)]
    all_to_all x0 -> x1, starting transfers between devices: none -> 7.21 us  [per_device(): lax.all_to_all(jnp.stack([centres] * lax.axis_size('ao')), 'ao', 0, 0)]
    ppermute x8, waiting for transfers between devices: 20.2 us -> 25.2 us  [shifted(): return lax.ppermute(block, axis, route)]
    ppermute x8, starting transfers between devices: 34.4 us -> 36.1 us  [shifted(): return lax.ppermute(block, axis, route)]
    another operation x0 -> x1, local copies, waits for them, and re-layouts: none -> 1.55 us  [per_device(): jnp.stack([centres] * lax.axis_size('ao'))]
    dot_general x5, matrix products: 25.1 us -> 24 us  [contribute(): return jnp.dot(kern, coef_rows, preferred_element_type=jnp.float32)]
  transfers between devices with their start and end apart: 8 -> 9, of which waited for: 3 -> 5; matrix products, arithmetic and copies ran while one was open for 21% -> 21% of each run, Pallas kernels for 0% -> 0%
where the time goes in v1:
time: 101 us; the launch traced here: 100 us
  starting transfers between devices  43.3 us (43%)
  waiting for transfers between devices  25.3 us (25%)
  matrix products  24 us (24%)
  between operations  3.33 us (3%)
  local copies, waits for them, and re-layouts  2.31 us (2%)
  other arithmetic  2.2 us (2%)
    ppermute x8, starting transfers between devices, shifted(): return lax.ppermute(block, axis, route)  36.1 us
    ppermute x8, waiting for transfers between devices, shifted(): return lax.ppermute(block, axis, route)  25.2 us
    dot_general x5, matrix products, contribute(): return jnp.dot(kern, coef_rows, preferred_element_type=jnp.float32)  24 us
    all_to_all x1, starting transfers between devices, per_device(): lax.all_to_all(jnp.stack([centres] * lax.axis_size('ao')), 'ao', 0, 0)  7.21 us
  transfers between devices with their start and end apart: 9, of which 5 were waited for; matrix products, arithmetic and copies ran while one was open for 21% of the time, Pallas kernels for 0%

profile of v1, /device:TPU:2, one launch (start us, length us, event | category | flops | bytes accessed | tf_op | source)
XLA Modules:
  0.0 100.4 jit_solution(10416559102916016629)
XLA Ops:
  0.0 0.0 copy-start
  0.0 0.0 copy-start.2
  0.0 0.0 copy-start.1
  0.0 1.5 %stack.2 = bf16[16,64,128]{2,1,0:T(8,128)(2,1)} broadcast(bf16[64,128]{1,0:T(8,128)(2,1)} %param.5), dimensions={1,2} | broadcast | bytes 278528 | tf_op jit(solution)/shard_map/stack | solution.py:44
  1.6 7.2 %all-to-all-start = ((bf16[16,64,128]{2,1,0:T(8,128)(2,1)}), bf16[16,64,128]{2,1,0:T(8,128)(2,1)S(1)}, u32[]{:S(2)}, u32[]{:S(2)}) async-start(bf16[16,64,128]{2,1,0:T(8,128)(2,1)} %stack.2), calls=%async_computation | async-start | bytes 524288 | tf_op jit(solution)/shard_map/all_to_all | solution.py:44
  8.8 4.3 %collective-permute-start.3 = (bf16[1024,256]{1,0:T(8,128)(2,1)}, bf16[1024,256]{1,0:T(8,128)(2,1)S(1)}, u32[]{:S(2)}, u32[]{:S(2)}) collective-permute-start(bf16[1024,256]{1,0:T(8,128)(2,1)} %param.6), channel_id=1, source_target_pairs={{0,16},{16,32},{32,48},{48,64},{64,80},{80,96},{96,112},{112,128},... | collective-permute-start | bytes 1572872 | tf_op jit(solution)/shard_map/ppermute | solution.py:13
  13.1 6.1 %collective-permute-start.1 = (bf16[1024,256]{1,0:T(8,128)(2,1)}, bf16[1024,256]{1,0:T(8,128)(2,1)S(1)}, u32[]{:S(2)}, u32[]{:S(2)}) collective-permute-start(bf16[1024,256]{1,0:T(8,128)(2,1)} %param.6), channel_id=1, source_target_pairs={{0,32},{16,48},{32,64},{48,80},{64,96},{80,112},{96,128},{112,144}... | collective-permute-start | bytes 1572872 | tf_op jit(solution)/shard_map/ppermute | solution.py:13
  19.2 0.0 copy-done
  19.2 0.1 constant_dynamic-slice_fusion
  19.3 0.6 fusion.50
  23.0 1.2 %multiply_reduce_fusion.5 = f32[1024]{0:T(1024)S(1)} fusion(bf16[1024,128]{1,0:T(8,128)(2,1)} %param.4), kind=kLoop, calls=%fused_computation.35 | loop fusion | flops 392192 | bytes 266240 | tf_op jit(solution)/shard_map/reduce_sum | solution.py:18
  24.2 0.0 all-to-all-done
  24.2 6.6 %collective-permute-start.6 = (bf16[1024,128]{1,0:T(8,128)(2,1)S(1)}, bf16[1024,128]{1,0:T(8,128)(2,1)S(1)}, u32[]{:S(2)}, u32[]{:S(2)}) collective-permute-start(bf16[1024,128]{1,0:T(8,128)(2,1)S(1)} %bitcast.21), channel_id=1, source_target_pairs={{32,0},{48,16},{64,32},{80,48},{96,64},{112,80},{128,96},{144,112}... | collective-permute-start | bytes 786440 | tf_op jit(solution)/shard_map/ppermute | solution.py:13
  30.9 2.6 %collective-permute-start.4 = (bf16[1024,128]{1,0:T(8,128)(2,1)S(1)}, bf16[1024,128]{1,0:T(8,128)(2,1)S(1)}, u32[]{:S(2)}, u32[]{:S(2)}) collective-permute-start(bf16[1024,128]{1,0:T(8,128)(2,1)S(1)} %bitcast.22), channel_id=1, source_target_pairs={{16,0},{32,16},{48,32},{64,48},{80,64},{96,80},{112,96},{128,112},... | collective-permute-start | bytes 786440 | tf_op jit(solution)/shard_map/ppermute | solution.py:13
  33.4 3.3 %collective-permute-start.2 = (bf16[1024,128]{1,0:T(8,128)(2,1)S(1)}, bf16[1024,128]{1,0:T(8,128)(2,1)S(1)}, u32[]{:S(2)}, u32[]{:S(2)}) collective-permute-start(bf16[1024,128]{1,0:T(8,128)(2,1)S(1)} %bitcast.23), channel_id=1, source_target_pairs={{0,16},{16,32},{32,48},{48,64},{64,80},{80,96},{96,112},{112,128},... | collective-permute-start | bytes 786440 | tf_op jit(solution)/shard_map/ppermute | solution.py:13
  36.7 0.2 multiply_reduce_fusion.4
  36.9 0.1 add.91
  37.0 0.0 copy-done.2
  37.0 0.0 copy-done.1
  37.0 4.0 %fusion.19 = f32[1024,256]{1,0:T(8,128)} fusion(bf16[1024,256]{1,0:T(8,128)(2,1)S(1)} %copy-done.2, bf16[1024,128]{1,0:T(8,128)(2,1)S(1)} %copy-done.1, bf16[1024,128]{1,0:T(8,128)(2,1)S(1)} %bitcast.24, f32[]{:T(128)} %bitcast.1, f32[1024]{0:T(1024)S(1)} %add.91, f32[1024]{0:T(1024)S(1)} %multiply_reduce_fusion.5), kind=kOutput, calls=%fused_computation.24 | convolution fusion | flops 819986432 | bytes 2105348 | tf_op jit(solution)/shard_map/dot_general | solution.py:35
  41.1 2.3 %collective-permute-done.6 = bf16[1024,128]{1,0:T(8,128)(2,1)S(1)} collective-permute-done((bf16[1024,128]{1,0:T(8,128)(2,1)S(1)}, bf16[1024,128]{1,0:T(8,128)(2,1)S(1)}, u32[]{:S(2)}, u32[]{:S(2)}) %collective-permute-start.6) | collective-permute-done | bytes 262176 | tf_op jit(solution)/shard_map/ppermute | solution.py:13
  43.4 5.7 %collective-permute-start = (bf16[1024,128]{1,0:T(8,128)(2,1)S(1)}, bf16[1024,128]{1,0:T(8,128)(2,1)S(1)}, u32[]{:S(2)}, u32[]{:S(2)}) collective-permute-start(bf16[1024,128]{1,0:T(8,128)(2,1)S(1)} %bitcast.25), channel_id=1, source_target_pairs={{0,32},{16,48},{32,64},{48,80},{64,96},{80,112},{96,128},{112,144}... | collective-permute-start | bytes 786440 | tf_op jit(solution)/shard_map/ppermute | solution.py:13
  49.1 0.2 multiply_reduce_fusion
  49.3 0.1 collective-permute-done.4
  49.5 3.2 %collective-permute-start.7 = (bf16[1024,256]{1,0:T(8,128)(2,1)S(1)}, bf16[1024,256]{1,0:T(8,128)(2,1)}, u32[]{:S(2)}, u32[]{:S(2)}) collective-permute-start(bf16[1024,256]{1,0:T(8,128)(2,1)S(1)} %copy-done.2), channel_id=1, source_target_pairs={{32,0},{48,16},{64,32},{80,48},{96,64},{112,80},{128,96},{144,112}... | collective-permute-start | bytes 1572872 | tf_op jit(solution)/shard_map/ppermute | solution.py:13
  52.7 0.2 multiply_reduce_fusion.1
  52.9 7.9 %collective-permute-done.2 = bf16[1024,128]{1,0:T(8,128)(2,1)S(1)} collective-permute-done((bf16[1024,128]{1,0:T(8,128)(2,1)S(1)}, bf16[1024,128]{1,0:T(8,128)(2,1)S(1)}, u32[]{:S(2)}, u32[]{:S(2)}) %collective-permute-start.2) | collective-permute-done | bytes 262176 | tf_op jit(solution)/shard_map/ppermute | solution.py:13
  60.8 4.3 %collective-permute-start.5 = (bf16[1024,256]{1,0:T(8,128)(2,1)S(1)}, bf16[1024,256]{1,0:T(8,128)(2,1)}, u32[]{:S(2)}, u32[]{:S(2)}) collective-permute-start(bf16[1024,256]{1,0:T(8,128)(2,1)S(1)} %copy-done.2), channel_id=1, source_target_pairs={{16,0},{32,16},{48,32},{64,48},{80,64},{96,80},{112,96},{128,112},... | collective-permute-start | bytes 1572872 | tf_op jit(solution)/shard_map/ppermute | solution.py:13
  65.2 0.2 multiply_reduce_fusion.2
  65.4 7.6 %collective-permute-done = bf16[1024,128]{1,0:T(8,128)(2,1)S(1)} collective-permute-done((bf16[1024,128]{1,0:T(8,128)(2,1)S(1)}, bf16[1024,128]{1,0:T(8,128)(2,1)S(1)}, u32[]{:S(2)}, u32[]{:S(2)}) %collective-permute-start) | collective-permute-done | bytes 262176 | tf_op jit(solution)/shard_map/ppermute | solution.py:13
  73.0 0.2 multiply_reduce_fusion.3
  73.2 0.0 collective-permute-done.3
  73.2 4.1 %fusion.17 = f32[1024,256]{1,0:T(8,128)} fusion(bf16[1024,256]{1,0:T(8,128)(2,1)S(1)} %collective-permute-done.3, bf16[1024,128]{1,0:T(8,128)(2,1)S(1)} %copy-done.1, bf16[1024,128]{1,0:T(8,128)(2,1)S(1)} %collective-permute-done.2, f32[]{:T(128)} %bitcast.3, f32[1024]{0:T(1024)S(1)} %multiply_reduce_fusion.2, f32[1024]{0:T(1024)S(1)} %multiply_reduce_fusion.5), kind=kOutput, calls=%fused_computation.22 | convolution fusion | flops 819986432 | bytes 2105348 | tf_op jit(solution)/shard_map/dot_general | solution.py:35
  77.3 0.0 collective-permute-done.7
  77.3 5.1 %fusion.15 = f32[1024,256]{1,0:T(8,128)} fusion(bf16[1024,256]{1,0:T(8,128)(2,1)} %collective-permute-done.7, bf16[1024,128]{1,0:T(8,128)(2,1)S(1)} %copy-done.1, bf16[1024,128]{1,0:T(8,128)(2,1)S(1)} %collective-permute-done.6, f32[]{:T(128)} %bitcast.5, f32[1024]{0:T(1024)S(1)} %multiply_reduce_fusion, f32[1024]{0:T(1024)S(1)} %multiply_reduce_fusion.5), kind=kOutput, calls=%fused_computation.20 | convolution fusion | flops 819986432 | bytes 2105348 | tf_op jit(solution)/shard_map/dot_general | solution.py:35
  82.4 7.2 %collective-permute-done.5 = bf16[1024,256]{1,0:T(8,128)(2,1)} collective-permute-done((bf16[1024,256]{1,0:T(8,128)(2,1)S(1)}, bf16[1024,256]{1,0:T(8,128)(2,1)}, u32[]{:S(2)}, u32[]{:S(2)}) %collective-permute-start.5) | collective-permute-done | bytes 524320 | tf_op jit(solution)/shard_map/ppermute | solution.py:13
  89.7 5.1 %fusion.16 = f32[1024,256]{1,0:T(8,128)} fusion(bf16[1024,256]{1,0:T(8,128)(2,1)} %collective-permute-done.5, bf16[1024,128]{1,0:T(8,128)(2,1)S(1)} %copy-done.1, bf16[1024,128]{1,0:T(8,128)(2,1)S(1)} %collective-permute-done.4, f32[]{:T(128)} %bitcast.4, f32[1024]{0:T(1024)S(1)} %multiply_reduce_fusion.1, f32[1024]{0:T(1024)S(1)} %multiply_reduce_fusion.5), kind=kOutput, calls=%fused_computation.21 | convolution fusion | flops 819986432 | bytes 2105348 | tf_op jit(solution)/shard_map/dot_general | solution.py:35
  94.8 0.0 collective-permute-done.1
  94.8 5.6 %fusion.24 = bf16[1024,256]{1,0:T(8,128)(2,1)} fusion(f32[1024,256]{1,0:T(8,128)} %fusion.15, f32[1024,256]{1,0:T(8,128)} %fusion.16, f32[1024,256]{1,0:T(8,128)} %fusion.17, f32[1024,256]{1,0:T(8,128)} %fusion.19, bf16[1024,256]{1,0:T(8,128)(2,1)S(1)} %collective-permute-done.1, bf16[1024,128]{1,0:T(8,128)(2,1)S(1)} %copy-done.1, ...), kind=kOutput, calls=%fused_computation.29 | convolution fusion | flops 821297152 | bytes 5775364 | tf_op jit(solution)/shard_map/dot_general | solution.py:35
Async XLA Ops:
  0.0 19.2 %copy-start = (s32[32,5]{0,1:T(8,128)S(1)}, s32[32,5]{0,1:T(8,128)}, u32[]{:S(2)}) copy-start(s32[32,5]{0,1:T(8,128)} %param.7) | copy-start | bytes 1924
  0.0 37.0 %copy-start.2 = (bf16[1024,256]{1,0:T(8,128)(2,1)S(1)}, bf16[1024,256]{1,0:T(8,128)(2,1)}, u32[]{:S(2)}) copy-start(bf16[1024,256]{1,0:T(8,128)(2,1)} %param.6) | copy-start | bytes 1572868
  0.0 37.0 %copy-start.1 = (bf16[1024,128]{1,0:T(8,128)(2,1)S(1)}, bf16[1024,128]{1,0:T(8,128)(2,1)}, u32[]{:S(2)}) copy-start(bf16[1024,128]{1,0:T(8,128)(2,1)} %param.4) | copy-start | bytes 786436
  1.6 22.7 %all-to-all-start = ((bf16[16,64,128]{2,1,0:T(8,128)(2,1)}), bf16[16,64,128]{2,1,0:T(8,128)(2,1)S(1)}, u32[]{:S(2)}, u32[]{:S(2)}) async-start(bf16[16,64,128]{2,1,0:T(8,128)(2,1)} %stack.2), calls=%async_computation | async-start | bytes 524288 | tf_op jit(solution)/shard_map/all_to_all | solution.py:44
  8.8 64.4 %collective-permute-start.3 = (bf16[1024,256]{1,0:T(8,128)(2,1)}, bf16[1024,256]{1,0:T(8,128)(2,1)S(1)}, u32[]{:S(2)}, u32[]{:S(2)}) collective-permute-start(bf16[1024,256]{1,0:T(8,128)(2,1)} %param.6), channel_id=1, source_target_pairs={{0,16},{16,32},{32,48},{48,64},{64,80},{80,96},{96,112},{112,128},... | collective-permute-start | bytes 1572872 | tf_op jit(solution)/shard_map/ppermute | solution.py:13
  13.1 81.7 %collective-permute-start.1 = (bf16[1024,256]{1,0:T(8,128)(2,1)}, bf16[1024,256]{1,0:T(8,128)(2,1)S(1)}, u32[]{:S(2)}, u32[]{:S(2)}) collective-permute-start(bf16[1024,256]{1,0:T(8,128)(2,1)} %param.6), channel_id=1, source_target_pairs={{0,32},{16,48},{32,64},{48,80},{64,96},{80,112},{96,128},{112,144}... | collective-permute-start | bytes 1572872 | tf_op jit(solution)/shard_map/ppermute | solution.py:13
  24.2 19.2 %collective-permute-start.6 = (bf16[1024,128]{1,0:T(8,128)(2,1)S(1)}, bf16[1024,128]{1,0:T(8,128)(2,1)S(1)}, u32[]{:S(2)}, u32[]{:S(2)}) collective-permute-start(bf16[1024,128]{1,0:T(8,128)(2,1)S(1)} %bitcast.21), channel_id=1, source_target_pairs={{32,0},{48,16},{64,32},{80,48},{96,64},{112,80},{128,96},{144,112}... | collective-permute-start | bytes 786440 | tf_op jit(solution)/shard_map/ppermute | solution.py:13
  30.9 18.6 %collective-permute-start.4 = (bf16[1024,128]{1,0:T(8,128)(2,1)S(1)}, bf16[1024,128]{1,0:T(8,128)(2,1)S(1)}, u32[]{:S(2)}, u32[]{:S(2)}) collective-permute-start(bf16[1024,128]{1,0:T(8,128)(2,1)S(1)} %bitcast.22), channel_id=1, source_target_pairs={{16,0},{32,16},{48,32},{64,48},{80,64},{96,80},{112,96},{128,112},... | collective-permute-start | bytes 786440 | tf_op jit(solution)/shard_map/ppermute | solution.py:13
  33.4 27.4 %collective-permute-start.2 = (bf16[1024,128]{1,0:T(8,128)(2,1)S(1)}, bf16[1024,128]{1,0:T(8,128)(2,1)S(1)}, u32[]{:S(2)}, u32[]{:S(2)}) collective-permute-start(bf16[1024,128]{1,0:T(8,128)(2,1)S(1)} %bitcast.23), channel_id=1, source_target_pairs={{0,16},{16,32},{32,48},{48,64},{64,80},{80,96},{96,112},{112,128},... | collective-permute-start | bytes 786440 | tf_op jit(solution)/shard_map/ppermute | solution.py:13
  43.4 29.6 %collective-permute-start = (bf16[1024,128]{1,0:T(8,128)(2,1)S(1)}, bf16[1024,128]{1,0:T(8,128)(2,1)S(1)}, u32[]{:S(2)}, u32[]{:S(2)}) collective-permute-start(bf16[1024,128]{1,0:T(8,128)(2,1)S(1)} %bitcast.25), channel_id=1, source_target_pairs={{0,32},{16,48},{32,64},{48,80},{64,96},{80,112},{96,128},{112,144}... | collective-permute-start | bytes 786440 | tf_op jit(solution)/shard_map/ppermute | solution.py:13
  49.5 27.9 %collective-permute-start.7 = (bf16[1024,256]{1,0:T(8,128)(2,1)S(1)}, bf16[1024,256]{1,0:T(8,128)(2,1)}, u32[]{:S(2)}, u32[]{:S(2)}) collective-permute-start(bf16[1024,256]{1,0:T(8,128)(2,1)S(1)} %copy-done.2), channel_id=1, source_target_pairs={{32,0},{48,16},{64,32},{80,48},{96,64},{112,80},{128,96},{144,112}... | collective-permute-start | bytes 1572872 | tf_op jit(solution)/shard_map/ppermute | solution.py:13
  60.8 28.9 %collective-permute-start.5 = (bf16[1024,256]{1,0:T(8,128)(2,1)S(1)}, bf16[1024,256]{1,0:T(8,128)(2,1)}, u32[]{:S(2)}, u32[]{:S(2)}) collective-permute-start(bf16[1024,256]{1,0:T(8,128)(2,1)S(1)} %copy-done.2), channel_id=1, source_target_pairs={{16,0},{32,16},{48,32},{64,48},{80,64},{96,80},{112,96},{128,112},... | collective-permute-start | bytes 1572872 | tf_op jit(solution)/shard_map/ppermute | solution.py:13
